TPU v7x, 256 devices: a whole 4x4x8 slice. The times are simulated.
256 devices in a mesh: dp: 8 (over x_hi, y), tensor: 32 (over z, x_lo, core).
Axes of the slice: x: 4 (x_hi: 2, x_lo: 2; x = x_hi * 2 + x_lo), y: 4, z: 8, core: 2. Of those that a mesh axis runs over, the one named last changes fastest.
Arguments:
- hidden: bfloat16 [4096, 16384], P('dp', 'tensor'), may hold values from -6 to 6
- down_weight: bfloat16 [16384, 8192], P('tensor'), may hold values from -0.046875 to 0.046875
- adapter_first_factor: bfloat16 [16384, 1024], P('tensor'), may hold values from -0.046875 to 0.046875
- adapter_second_factor: bfloat16 [1024, 8192], P(None, 'tensor'), may hold values from -1.5 to 1.5
- output_gradient: bfloat16 [4096, 8192], P(('dp', 'tensor')), may hold values from -6 to 6
- token_language_index: int32 [8, 512], P('dp'), may hold values from 0 to 63, never falling along the last dimension, each value on 1 to 128 neighbouring positions
- owned: int32 [64], replicated, may hold values from 0 to 63, each once
Outputs:
- mixed: bfloat16 [4096, 8192], P(('dp', 'tensor'))
- hidden_gradient: bfloat16 [4096, 16384], P('dp', 'tensor')
- grad_a: float32 [64, 16, 16384], P('dp', None, 'tensor')
- grad_b: float32 [64, 16, 8192], P('dp', None, 'tensor')
Inputs may be any that keep to these rules, and one draw needn't show every extreme that they name: Each row of token_language_index never falls and names every language; one language has exactly 128 tokens of the row, none more. `owned`: each adapter appears once.
All inputs are finite; a program needn't handle non-finite values.
Results may differ from a plain program's by a relative error of at most 0.0075.
Values may be sent and summed in bfloat16 or wider, within the bound.
A program may use at most 128 MiB of HBM per device.

v0:
```python
import jax
import jax.numpy as jnp
from jax import lax
from jax.sharding import PartitionSpec as P

ADAPTER_RANK = 16
LANGUAGE_COUNT = 64
adapter_scale = 0.5


def select_language_rank(full, language_mask):
    rows = full.shape[0]
    return jnp.sum(
        full.reshape(rows, LANGUAGE_COUNT, ADAPTER_RANK) * language_mask[:, :, None], axis=1
    )


def spread_rank(small, onehot_half):
    rows = small.shape[0]
    return (onehot_half[:, :, None] * small.astype(jnp.bfloat16)[:, None, :]).reshape(
        rows, LANGUAGE_COUNT * ADAPTER_RANK
    )


def contract_matrices(left, right, left_dim, right_dim):
    return lax.dot_general(
        left, right, (((left_dim,), (right_dim,)), ((), ())), preferred_element_type=jnp.float32
    )


def body(
    hidden,
    down_weight,
    adapter_first_factor,
    adapter_second_factor,
    output_gradient,
    token_language_index,
    owned,
):
    column_share = adapter_second_factor.shape[1]
    col_start = lax.axis_index("tensor") * column_share
    labels = token_language_index.reshape(-1)
    language_mask = (
        labels[:, None] == jnp.arange(LANGUAGE_COUNT, dtype=jnp.int32)[None, :]
    ).astype(jnp.float32)
    onehot_half = language_mask.astype(jnp.bfloat16)
    gathered = lax.all_gather(output_gradient, "tensor", axis=0, tiled=True)
    gradient_column_block = lax.dynamic_slice_in_dim(gathered, col_start, column_share, 1)
    frozen_input_gradient = contract_matrices(gathered, down_weight, 1, 1)
    rank_reduce_share = select_language_rank(
        jnp.dot(hidden, adapter_first_factor, preferred_element_type=jnp.float32), language_mask
    )
    input_gradient_share = select_language_rank(
        contract_matrices(gradient_column_block, adapter_second_factor, 1, 1), language_mask
    )
    rank_reduce, input_gradient = lax.psum((rank_reduce_share, input_gradient_share), "tensor")
    expanded_rank = spread_rank(rank_reduce, onehot_half)
    gradient_spread_rank = spread_rank(input_gradient, onehot_half)
    rank_expand = adapter_scale * jnp.dot(
        expanded_rank, adapter_second_factor, preferred_element_type=jnp.float32
    )
    base_rows = lax.psum_scatter(
        jnp.dot(hidden, down_weight, preferred_element_type=jnp.float32),
        "tensor",
        scatter_dimension=0,
        tiled=True,
    )
    lift_rows = lax.all_to_all(rank_expand, "tensor", split_axis=0, concat_axis=1, tiled=True)
    mixed = (base_rows + lift_rows).astype(jnp.bfloat16)
    hidden_gradient = (
        frozen_input_gradient
        + adapter_scale * contract_matrices(gradient_spread_rank, adapter_first_factor, 1, 1)
    ).astype(jnp.bfloat16)
    resident_first_factor = adapter_scale * contract_matrices(gradient_spread_rank, hidden, 0, 0)
    resident_second_factor = adapter_scale * contract_matrices(
        expanded_rank, gradient_column_block, 0, 0
    )
    ordered_a = jnp.take(
        resident_first_factor.reshape(LANGUAGE_COUNT, ADAPTER_RANK, -1), owned, axis=0
    )
    ordered_b = jnp.take(
        resident_second_factor.reshape(LANGUAGE_COUNT, ADAPTER_RANK, -1), owned, axis=0
    )
    grad_a, grad_b = (
        lax.psum_scatter(ordered_a, "dp", scatter_dimension=0, tiled=True),
        lax.psum_scatter(ordered_b, "dp", scatter_dimension=0, tiled=True),
    )
    return (mixed, hidden_gradient, grad_a, grad_b)


def solution(mesh):
    in_specs = (
        P("dp", "tensor"),
        P("tensor", None),
        P("tensor", None),
        P(None, "tensor"),
        P(("dp", "tensor"), None),
        P("dp", None),
        P(),
    )
    out_specs = (
        P(("dp", "tensor"), None),
        P("dp", "tensor"),
        P("dp", None, "tensor"),
        P("dp", None, "tensor"),
    )
    return jax.shard_map(body, mesh=mesh, in_specs=in_specs, out_specs=out_specs, check_vma=False)
```

profile of v0, /device:TPU:32, one launch (start us, length us, event | category | flops | bytes accessed | tf_op | source)
XLA Modules:
  0.0 457.7 jit_solution(10031234196702321765)
XLA Ops:
  7.2 0.0 copy-start
  7.2 0.0 all-gather.2.cloned.1.call-start
  7.2 0.7 all-gather.2.cloned.1.call-update
  7.9 0.0 reduce-scatter.4.cloned.1.call-start
  8.0 13.8 %fusion.9 = f32[512,8192]{1,0:T(8,128)} fusion(bf16[512,512]{1,0:T(8,128)(2,1)} %param.7, bf16[512,8192]{1,0:T(8,128)(2,1)} %param.8), kind=kOutput, calls=%fused_computation.26 | convolution fusion | flops 4294967296 | bytes 25690112 | tf_op jit(solution)/shard_map/dot_general | solution.py:63
  21.8 0.0 copy-start.9
  21.8 0.0 copy-start.1
  21.8 0.0 reduce-scatter.4.cloned.1.call-update
  21.8 0.0 copy-start.7
  21.8 0.0 reduce-scatter.8.cloned.1.call-start
  21.9 0.6 copy-done.10
  22.5 0.0 copy-done.9
  22.5 0.0 copy-done
  22.5 0.3 copy-done.1
  22.9 2.1 fusion.10
  25.0 59.6 %all-gather.2.cloned.1.call-done = bf16[512,8192]{1,0:T(8,128)(2,1)} async-done(((bf16[16,8192]{1,0:T(8,128)(2,1)}), bf16[512,8192]{1,0:T(8,128)(2,1)}) %all-gather.2.cloned.1.call-update) | async-done | bytes 8388624 | tf_op jit(solution)/shard_map/all_gather | solution.py:47
  84.6 0.0 copy-done.7
  84.6 1.6 fusion.3
  86.1 0.1 copy-done.2
  86.2 0.7 multiply_reduce_fusion
  86.9 102.4 %all-reduce = (bf16[512,16]{0,1:T(8,128)(2,1)S(1)}, bf16[512,16]{0,1:T(8,128)(2,1)S(1)}) all-reduce(f32[512,16]{0,1:T(8,128)S(1)} %get-tuple-element.5, f32[512,16]{0,1:T(8,128)S(1)} %get-tuple-element.4), channel_id=1, replica_groups=mesh['dp'=8,'tensor'=32] {'tensor'}, use_global_device_ids=true, to_apply=%region_2.0 | all-reduce | flops 16384 | bytes 98304 | tf_op jit(solution)/shard_map/psum | solution.py:56
  189.3 0.1 broadcast_multiply_fusion
  189.4 0.0 copy-start.5
  189.5 0.0 copy-start.3
  189.5 1.0 copy-done.5
  190.4 2.5 convolution_multiply_fusion.2
  192.9 2.9 gather_fusion.1
  195.8 2.4 broadcast_select_fusion.1
  198.2 0.0 reduce-scatter.8.cloned.1.call-update
  198.3 0.0 reduce-scatter.6.cloned.1.call-start
  198.3 0.0 copy-done.3
  198.3 2.1 convolution_multiply_fusion
  200.4 2.3 gather_fusion
  202.7 1.6 broadcast_select_fusion
  204.3 0.0 reduce-scatter.6.cloned.1.call-update
  204.3 1.2 copy-done.6
  205.5 0.1 copy-done.8
  205.6 1.3 convolution_multiply_fusion.3
  206.9 12.0 %all-to-all-start = ((f32[32,16,256]{2,1,0:T(8,128)}), f32[32,16,256]{2,1,0:T(8,128)S(1)}, u32[]{:S(2)}, u32[]{:S(2)}) async-start(f32[32,16,256]{2,1,0:T(8,128)} %bitcast.3), calls=%async_computation.1 | async-start | bytes 1048576 | tf_op jit(solution)/shard_map/all_to_all | solution.py:68
  218.9 0.0 copy-start.4
  218.9 9.7 %fusion.11 = f32[512,512]{1,0:T(8,128)S(1)} fusion(bf16[512,8192]{1,0:T(8,128)(2,1)} %all-gather.2.cloned.1.call-done, bf16[512,8192]{1,0:T(8,128)(2,1)} %param.8), kind=kOutput, calls=%fused_computation.28 | convolution fusion | flops 4294967296 | bytes 17825792 | tf_op jit(solution)/shard_map/dot_general | solution.py:26
  228.6 0.0 copy-done.4
  228.7 1.6 fusion.1
  230.2 8.5 %all-to-all-done = f32[32,16,256]{2,1,0:T(8,128)S(1)} async-done(((f32[32,16,256]{2,1,0:T(8,128)}), f32[32,16,256]{2,1,0:T(8,128)S(1)}, u32[]{:S(2)}, u32[]{:S(2)}) %all-to-all-start) | async-done | bytes 524320 | tf_op jit(solution)/shard_map/all_to_all | solution.py:68
  238.7 43.1 %reduce-scatter.4.cloned.1.call-done = f32[16,8192]{1,0:T(8,128)} async-done(((f32[512,8192]{1,0:T(8,128)}), f32[16,8192]{1,0:T(8,128)}) %reduce-scatter.4.cloned.1.call-update) | async-done | bytes 524304 | tf_op jit(solution)/shard_map/reduce_scatter | solution.py:62
  281.8 1.8 add_convert_fusion
  283.6 83.4 %reduce-scatter.8.cloned.1.call-done = f32[8,16,256]{2,1,0:T(8,128)} async-done(((f32[64,16,256]{2,1,0:T(8,128)}), f32[8,16,256]{2,1,0:T(8,128)}) %reduce-scatter.8.cloned.1.call-update) | async-done | bytes 131088 | tf_op jit(solution)/shard_map/reduce_scatter | solution.py:86
  367.0 84.2 %reduce-scatter.6.cloned.1.call-done = f32[8,16,512]{2,1,0:T(8,128)} async-done(((f32[64,16,512]{2,1,0:T(8,128)}), f32[8,16,512]{2,1,0:T(8,128)}) %reduce-scatter.6.cloned.1.call-update) | async-done | bytes 262160 | tf_op jit(solution)/shard_map/reduce_scatter | solution.py:85
  (9 shorter events, 0.1 us)
Async XLA Ops:
  7.2 15.4 %copy-start = (bf16[512,1024]{1,0:T(8,128)(2,1)S(1)}, bf16[512,1024]{1,0:T(8,128)(2,1)}, u32[]{:S(2)}) copy-start(bf16[512,1024]{1,0:T(8,128)(2,1)} %param.9) | copy-start | bytes 3145732
  7.2 77.4 %all-gather.2.cloned.1.call-start = ((), (), s32[]{:S(2)}) async-start(), calls=%async_computation.5 | async-start | bytes 8650752 | tf_op jit(solution)/shard_map/all_gather | solution.py:47
  7.9 273.9 %reduce-scatter.4.cloned.1.call-start = ((), (), s32[]{:S(2)}) async-start(), calls=%async_computation.4 | async-start | bytes 17301504 | tf_op jit(solution)/shard_map/reduce_scatter | solution.py:62
  21.8 0.7 copy-start.10
  21.8 0.7 copy-start.9
  21.8 1.1 copy-start.1
  21.8 62.7 %copy-start.7 = (bf16[1024,256]{1,0:T(8,128)(2,1)S(1)}, bf16[1024,256]{1,0:T(8,128)(2,1)}, u32[]{:S(2)}) copy-start(bf16[1024,256]{1,0:T(8,128)(2,1)} %param.10) | copy-start | bytes 1572868
  21.8 345.2 %reduce-scatter.8.cloned.1.call-start = ((), (), s32[]{:S(2)}) async-start(), calls=%async_computation.7 | async-start | bytes 1179648 | tf_op jit(solution)/shard_map/reduce_scatter | solution.py:86
  84.6 1.7 copy-start.2
  189.4 1.0 copy-start.5
  189.5 8.9 %copy-start.3 = (bf16[512,64,16]{0,2,1:T(8,128)(2,1)}, bf16[512,64,16]{0,2,1:T(8,128)(2,1)S(1)}, u32[]{:S(2)}) copy-start(bf16[512,64,16]{0,2,1:T(8,128)(2,1)S(1)} %get-tuple-element.8) | copy-start | bytes 3145732
  198.3 252.9 %reduce-scatter.6.cloned.1.call-start = ((), (), s32[]{:S(2)}) async-start(), calls=%async_computation.6 | async-start | bytes 2359296 | tf_op jit(solution)/shard_map/reduce_scatter | solution.py:85
  204.3 1.2 copy-start.6
  204.3 1.4 copy-start.8
  206.9 31.8 %all-to-all-start = ((f32[32,16,256]{2,1,0:T(8,128)}), f32[32,16,256]{2,1,0:T(8,128)S(1)}, u32[]{:S(2)}, u32[]{:S(2)}) async-start(f32[32,16,256]{2,1,0:T(8,128)} %bitcast.3), calls=%async_computation.1 | async-start | bytes 1048576 | tf_op jit(solution)/shard_map/all_to_all | solution.py:68
  218.9 9.8 %copy-start.4 = (bf16[512,64,16]{0,2,1:T(8,128)(2,1)S(1)}, bf16[512,64,16]{0,2,1:T(8,128)(2,1)}, u32[]{:S(2)}) copy-start(bf16[512,64,16]{0,2,1:T(8,128)(2,1)} %copy-done.3) | copy-start | bytes 3145732
Sparse Core Ops, SparseCore 0:
  9.9 74.6 all-gather.1
  87.1 194.6 reduce-scatter.3
  286.3 80.6 reduce-scatter.7
  372.0 79.1 reduce-scatter.5
where the time goes:
time: 458 us
  waiting for transfers between devices  279 us (61%)
  blocking collectives  102 us (22%)
  matrix products  34.6 us (8%)
  between operations  13.9 us (3%)
  starting transfers between devices  12.1 us (3%)
  local copies, waits for them, and re-layouts  8.59 us (2%)
  other arithmetic  6.66 us (1%)
    psum x1, blocking collectives, body(): lax.psum((rank_reduce_share, input_gradient_share), 'tensor')  102 us
    reduce_scatter x1, waiting for transfers between devices, body(): lax.psum_scatter(ordered_a, 'dp', scatter_dimension=0, tiled=True)  84.2 us
    reduce_scatter x1, waiting for transfers between devices, body(): lax.psum_scatter(ordered_b, 'dp', scatter_dimension=0, tiled=True)  83.4 us
    all_gather x1, waiting for transfers between devices, body(): gathered = lax.all_gather(output_gradient, 'tensor', axis=0, tiled=True)  59.6 us
    reduce_scatter x1, waiting for transfers between devices, body(): lax.psum_scatter(jnp.dot(hidden, down_weight, preferred_element_type=jnp....  43.1 us
    dot_general x5, matrix products, contract_matrices(): lax.dot_general(left, right, (((left_dim,), (right_dim,)), ((), ())), pre...  17.4 us
    dot_general x1, matrix products, body(): jnp.dot(hidden, down_weight, preferred_element_type=jnp.float32)  13.8 us
    all_to_all x1, starting transfers between devices, body(): lax.all_to_all(rank_expand, 'tensor', split_axis=0, concat_axis=1, tiled=...  12 us
  transfers between devices with their start and end apart: 5, of which 5 were waited for; matrix products, arithmetic and copies ran while one was open for 10% of the time, Pallas kernels for 0%

commit v1 on v0

--- a/solution.py
+++ b/solution.py
@@ -44,7 +44,10 @@
         labels[:, None] == jnp.arange(LANGUAGE_COUNT, dtype=jnp.int32)[None, :]
     ).astype(jnp.float32)
     onehot_half = language_mask.astype(jnp.bfloat16)
-    gathered = lax.all_gather(output_gradient, "tensor", axis=0, tiled=True)
+    gathered = jnp.concatenate(
+        lax.all_to_all(jnp.stack([output_gradient] * lax.axis_size("tensor")), "tensor", 0, 0),
+        axis=0,
+    )
     gradient_column_block = lax.dynamic_slice_in_dim(gathered, col_start, column_share, 1)
     frozen_input_gradient = contract_matrices(gathered, down_weight, 1, 1)
     rank_reduce_share = select_language_rank(

time: 458 us -> 547 us (1.19)
  waiting for transfers between devices: 279 us -> 357 us
  starting transfers between devices: 12.1 us -> 21.1 us
    all_to_all x0 -> x1, waiting for transfers between devices: none -> 226 us  [body(): lax.all_to_all(jnp.stack([output_gradient] * lax.axis_size('tensor')), 't...]
    all_gather x1 -> x0, waiting for transfers between devices: 59.6 us -> none  [body(): gathered = lax.all_gather(output_gradient, 'tensor', axis=0, tiled=True)]
    reduce_scatter x1, waiting for transfers between devices: 43.1 us -> 0.02 us  [body(): lax.psum_scatter(jnp.dot(hidden, down_weight, preferred_element_type=jnp....]
    reduce_scatter x1, waiting for transfers between devices: 83.4 us -> 40.8 us  [body(): lax.psum_scatter(ordered_b, 'dp', scatter_dimension=0, tiled=True)]
    all_to_all x0 -> x1, starting transfers between devices: none -> 9.84 us  [body(): lax.all_to_all(jnp.stack([output_gradient] * lax.axis_size('tensor')), 't...]
  transfers between devices with their start and end apart: 5 -> 5, of which waited for: 5 -> 4; matrix products, arithmetic and copies ran while one was open for 10% -> 7% of each run, Pallas kernels for 0% -> 0%
where the time goes in v1:
time: 547 us
  waiting for transfers between devices  357 us (65%)
  blocking collectives  101 us (18%)
  matrix products  34.5 us (6%)
  starting transfers between devices  21.1 us (4%)
  between operations  13.9 us (3%)
  local copies, waits for them, and re-layouts  12.8 us (2%)
  other arithmetic  6.64 us (1%)
    all_to_all x1, waiting for transfers between devices, body(): lax.all_to_all(jnp.stack([output_gradient] * lax.axis_size('tensor')), 't...  226 us
    psum x1, blocking collectives, body(): lax.psum((rank_reduce_share, input_gradient_share), 'tensor')  101 us
    reduce_scatter x1, waiting for transfers between devices, body(): lax.psum_scatter(ordered_a, 'dp', scatter_dimension=0, tiled=True)  84.2 us
    reduce_scatter x1, waiting for transfers between devices, body(): lax.psum_scatter(ordered_b, 'dp', scatter_dimension=0, tiled=True)  40.8 us
    dot_general x5, matrix products, contract_matrices(): lax.dot_general(left, right, (((left_dim,), (right_dim,)), ((), ())), pre...  17.3 us
    dot_general x1, matrix products, body(): jnp.dot(hidden, down_weight, preferred_element_type=jnp.float32)  13.9 us
    all_to_all x1, starting transfers between devices, body(): lax.all_to_all(rank_expand, 'tensor', split_axis=0, concat_axis=1, tiled=...  11.1 us
  transfers between devices with their start and end apart: 5, of which 4 were waited for; matrix products, arithmetic and copies ran while one was open for 7% of the time, Pallas kernels for 0%

profile of v1, /device:TPU:32, one launch (start us, length us, event | category | flops | bytes accessed | tf_op | source)
XLA Modules:
  0.0 546.7 jit_solution(292505652331290079)
XLA Ops:
  7.2 0.0 copy-start
  7.2 0.0 reduce-scatter.4.cloned.1.call-start
  7.2 13.9 %fusion.9 = f32[512,8192]{1,0:T(8,128)} fusion(bf16[512,512]{1,0:T(8,128)(2,1)} %param.7, bf16[512,8192]{1,0:T(8,128)(2,1)} %param.8), kind=kOutput, calls=%fused_computation.26 | convolution fusion | flops 4294967296 | bytes 25690112 | tf_op jit(solution)/shard_map/dot_general | solution.py:66
  21.1 0.0 copy-start.9
  21.1 0.0 reduce-scatter.4.cloned.1.call-update
  21.2 0.9 copy-done.9
  22.1 4.2 stack.2
  26.3 9.8 %all-to-all-start.1 = ((bf16[32,16,8192]{2,1,0:T(8,128)(2,1)}), bf16[32,16,8192]{2,1,0:T(8,128)(2,1)}, u32[]{:S(2)}, u32[]{:S(2)}) async-start(bf16[32,16,8192]{2,1,0:T(8,128)(2,1)} %stack.2), calls=%async_computation.2 | async-start | bytes 16777216 | tf_op jit(solution)/shard_map/all_to_all | solution.py:48
  36.2 0.0 copy-start.7
  36.2 0.0 reduce-scatter.8.cloned.1.call-start
  36.2 0.0 copy-done.11
  36.3 0.0 copy-done.10
  36.3 0.0 copy-done
  36.3 0.0 copy-done.1
  36.3 2.1 fusion.10
  38.4 225.8 %all-to-all-done.1 = bf16[32,16,8192]{2,1,0:T(8,128)(2,1)} async-done(((bf16[32,16,8192]{2,1,0:T(8,128)(2,1)}), bf16[32,16,8192]{2,1,0:T(8,128)(2,1)}, u32[]{:S(2)}, u32[]{:S(2)}) %all-to-all-start.1) | async-done | bytes 8388640 | tf_op jit(solution)/shard_map/all_to_all | solution.py:48
  264.2 0.0 copy-done.7
  264.2 1.6 fusion.3
  265.8 0.1 copy-done.2
  265.9 0.7 multiply_reduce_fusion
  266.6 101.2 %all-reduce = (bf16[512,16]{0,1:T(8,128)(2,1)S(1)}, bf16[512,16]{0,1:T(8,128)(2,1)S(1)}) all-reduce(f32[512,16]{0,1:T(8,128)S(1)} %get-tuple-element.5, f32[512,16]{0,1:T(8,128)S(1)} %get-tuple-element.4), channel_id=1, replica_groups=mesh['dp'=8,'tensor'=32] {'tensor'}, use_global_device_ids=true, to_apply=%region_2.0 | all-reduce | flops 16384 | bytes 98304 | tf_op jit(solution)/shard_map/psum | solution.py:59
  367.8 0.1 broadcast_multiply_fusion
  367.9 0.0 copy-start.5
  367.9 0.0 copy-start.3
  367.9 1.0 copy-done.5
  368.9 2.4 convolution_multiply_fusion.2
  371.4 2.9 gather_fusion.1
  374.3 2.4 broadcast_select_fusion.1
  376.7 0.0 reduce-scatter.8.cloned.1.call-update
  376.7 0.0 reduce-scatter.6.cloned.1.call-start
  376.7 0.0 copy-done.3
  376.8 2.1 convolution_multiply_fusion
  378.8 2.3 gather_fusion
  381.1 1.6 broadcast_select_fusion
  382.7 0.0 reduce-scatter.6.cloned.1.call-update
  382.7 1.2 copy-done.6
  383.9 0.1 copy-done.8
  384.1 1.3 convolution_multiply_fusion.3
  385.3 11.1 %all-to-all-start = ((f32[32,16,256]{2,1,0:T(8,128)}), f32[32,16,256]{2,1,0:T(8,128)S(1)}, u32[]{:S(2)}, u32[]{:S(2)}) async-start(f32[32,16,256]{2,1,0:T(8,128)} %bitcast.3), calls=%async_computation.1 | async-start | bytes 1048576 | tf_op jit(solution)/shard_map/all_to_all | solution.py:71
  396.4 0.0 copy-start.4
  396.5 9.6 %fusion.11 = f32[512,512]{1,0:T(8,128)S(1)} fusion(bf16[512,8192]{1,0:T(8,128)(2,1)} %bitcast.5, bf16[512,8192]{1,0:T(8,128)(2,1)} %param.8), kind=kOutput, calls=%fused_computation.28 | convolution fusion | flops 4294967296 | bytes 17825792 | tf_op jit(solution)/shard_map/dot_general | solution.py:26
  406.1 0.0 copy-done.4
  406.1 1.6 fusion.1
  407.6 5.6 %all-to-all-done = f32[32,16,256]{2,1,0:T(8,128)S(1)} async-done(((f32[32,16,256]{2,1,0:T(8,128)}), f32[32,16,256]{2,1,0:T(8,128)S(1)}, u32[]{:S(2)}, u32[]{:S(2)}) %all-to-all-start) | async-done | bytes 524320 | tf_op jit(solution)/shard_map/all_to_all | solution.py:71
  413.3 0.0 reduce-scatter.4.cloned.1.call-done
  413.3 1.8 add_convert_fusion
  415.1 40.8 %reduce-scatter.8.cloned.1.call-done = f32[8,16,256]{2,1,0:T(8,128)} async-done(((f32[64,16,256]{2,1,0:T(8,128)}), f32[8,16,256]{2,1,0:T(8,128)}) %reduce-scatter.8.cloned.1.call-update) | async-done | bytes 131088 | tf_op jit(solution)/shard_map/reduce_scatter | solution.py:89
  456.0 84.2 %reduce-scatter.6.cloned.1.call-done = f32[8,16,512]{2,1,0:T(8,128)} async-done(((f32[64,16,512]{2,1,0:T(8,128)}), f32[8,16,512]{2,1,0:T(8,128)}) %reduce-scatter.6.cloned.1.call-update) | async-done | bytes 262160 | tf_op jit(solution)/shard_map/reduce_scatter | solution.py:88
  (11 shorter events, 0.1 us)
Async XLA Ops:
  7.2 29.2 %copy-start = (bf16[512,1024]{1,0:T(8,128)(2,1)S(1)}, bf16[512,1024]{1,0:T(8,128)(2,1)}, u32[]{:S(2)}) copy-start(bf16[512,1024]{1,0:T(8,128)(2,1)} %param.9) | copy-start | bytes 3145732
  7.2 406.1 %reduce-scatter.4.cloned.1.call-start = ((), (), s32[]{:S(2)}) async-start(), calls=%async_computation.5 | async-start | bytes 17301504 | tf_op jit(solution)/shard_map/reduce_scatter | solution.py:65
  21.1 0.9 copy-start.9
  26.3 9.9 %copy-start.11 = (s32[64]{0:T(128)S(1)}, s32[64]{0:T(128)}, u32[]{:S(2)}) copy-start(s32[64]{0:T(128)} %param.13) | copy-start | bytes 772
  26.3 10.0 %copy-start.10 = (s32[1,512]{1,0:T(1,128)S(1)}, s32[1,512]{1,0:T(1,128)}, u32[]{:S(2)}) copy-start(s32[1,512]{1,0:T(1,128)} %param.12) | copy-start | bytes 6148
  26.3 10.0 %copy-start.1 = (bf16[512,512]{1,0:T(8,128)(2,1)S(1)}, bf16[512,512]{1,0:T(8,128)(2,1)}, u32[]{:S(2)}) copy-start(bf16[512,512]{1,0:T(8,128)(2,1)} %param.7) | copy-start | bytes 1572868
  26.3 237.9 %all-to-all-start.1 = ((bf16[32,16,8192]{2,1,0:T(8,128)(2,1)}), bf16[32,16,8192]{2,1,0:T(8,128)(2,1)}, u32[]{:S(2)}, u32[]{:S(2)}) async-start(bf16[32,16,8192]{2,1,0:T(8,128)(2,1)} %stack.2), calls=%async_computation.2 | async-start | bytes 16777216 | tf_op jit(solution)/shard_map/all_to_all | solution.py:48
  36.2 228.1 %copy-start.7 = (bf16[1024,256]{1,0:T(8,128)(2,1)S(1)}, bf16[1024,256]{1,0:T(8,128)(2,1)}, u32[]{:S(2)}) copy-start(bf16[1024,256]{1,0:T(8,128)(2,1)} %param.10) | copy-start | bytes 1572868
  36.2 419.8 %reduce-scatter.8.cloned.1.call-start = ((), (), s32[]{:S(2)}) async-start(), calls=%async_computation.7 | async-start | bytes 1179648 | tf_op jit(solution)/shard_map/reduce_scatter | solution.py:89
  264.2 1.7 copy-start.2
  367.9 1.0 copy-start.5
  367.9 8.8 %copy-start.3 = (bf16[512,64,16]{0,2,1:T(8,128)(2,1)}, bf16[512,64,16]{0,2,1:T(8,128)(2,1)S(1)}, u32[]{:S(2)}) copy-start(bf16[512,64,16]{0,2,1:T(8,128)(2,1)S(1)} %get-tuple-element.8) | copy-start | bytes 3145732
  376.7 163.5 %reduce-scatter.6.cloned.1.call-start = ((), (), s32[]{:S(2)}) async-start(), calls=%async_computation.6 | async-start | bytes 2359296 | tf_op jit(solution)/shard_map/reduce_scatter | solution.py:88
  382.7 1.2 copy-start.6
  382.7 1.4 copy-start.8
  385.3 27.9 %all-to-all-start = ((f32[32,16,256]{2,1,0:T(8,128)}), f32[32,16,256]{2,1,0:T(8,128)S(1)}, u32[]{:S(2)}, u32[]{:S(2)}) async-start(f32[32,16,256]{2,1,0:T(8,128)} %bitcast.3), calls=%async_computation.1 | async-start | bytes 1048576 | tf_op jit(solution)/shard_map/all_to_all | solution.py:71
  396.4 9.6 %copy-start.4 = (bf16[512,64,16]{0,2,1:T(8,128)(2,1)S(1)}, bf16[512,64,16]{0,2,1:T(8,128)(2,1)}, u32[]{:S(2)}) copy-start(bf16[512,64,16]{0,2,1:T(8,128)(2,1)} %copy-done.3) | copy-start | bytes 3145732
Sparse Core Ops, SparseCore 0:
  21.3 325.2 reduce-scatter.3
  376.8 79.0 reduce-scatter.7
  461.1 79.0 reduce-scatter.5
